TPU v7x, 256 devices: a whole 4x4x8 slice. The times are simulated.
256 devices in a mesh: br: 64 (over z, y_hi, x), bus: 4 (over y_lo, core).
Axes of the slice: x: 4, y: 4 (y_hi: 2, y_lo: 2; y = y_hi * 2 + y_lo), z: 8, core: 2. Of those that a mesh axis runs over, the one named last changes fastest.
Arguments:
- net_load: bfloat16 [128, 60416], P('br', 'bus'), may hold values from -6 to 6
- release: float32 [128, 1024], P('br'), may hold values from 0 to 2
- plant_bus: int32 [1024], replicated, may hold values from 0 to 60415
- efficiency: float32 [1024], replicated, may hold values from 0.5 to 2
- ptdf: bfloat16 [8192, 60416], P('br', 'bus'), may hold values from -0.0234375 to 0.0234375
- branch_class: int32 [8192], P('br'), may hold values from 0 to 15
- class_limit: float32 [16], replicated, may hold values from 0.4 to 3
- class_price: float32 [16], replicated, may hold values from 0.5 to 5
Outputs:
- grad_bus: float32 [128, 60416], P('br', 'bus')
- grad_release: float32 [128, 1024], P('br')
All inputs are finite; a program needn't handle non-finite values.
Results may differ from a plain program's by a relative error of at most 0.0031.
Values may be sent and summed in bfloat16 or wider, within the bound.
A program may use at most 64 MiB of HBM per device.

v0:
```python
import jax
import jax.numpy as jnp
from jax import lax
from jax.sharding import PartitionSpec as P

SMOOTH = 0.25


def shards(net_load, release, plant_bus, efficiency, ptdf, branch_class, class_limit, class_price):
    rows_local, bus_local = net_load.shape
    offset = lax.axis_index("bus") * bus_local
    columns = plant_bus - offset
    inside = ((columns >= 0) & (columns < bus_local)).astype(jnp.float32)
    clipped = jnp.clip(columns, 0, bus_local - 1)
    weighted = efficiency * inside
    inject = (
        net_load.astype(jnp.float32)
        .at[:, clipped]
        .add(release * weighted[None, :])
        .astype(jnp.bfloat16)
    )
    partial_flows = lax.dot_general(
        lax.all_gather(inject, "br", axis=0, tiled=True),
        ptdf,
        (((1,), (1,)), ((), ())),
        preferred_element_type=jnp.float32,
    )
    onehot = (branch_class[:, None] == jnp.arange(class_limit.shape[0])[None, :]).astype(
        jnp.float32
    )
    limit = jnp.sum(onehot * class_limit[None, :], axis=1)[None, :]
    price = jnp.sum(onehot * class_price[None, :], axis=1)[None, :]
    flows = lax.psum(partial_flows, "bus")
    upper = jax.nn.sigmoid((flows - limit) / SMOOTH)
    lower = jax.nn.sigmoid((-flows - limit) / SMOOTH)
    grad_flow = (price * (upper - lower)).astype(jnp.bfloat16)
    grad_bus = lax.psum_scatter(
        jnp.dot(grad_flow, ptdf, preferred_element_type=jnp.float32),
        "br",
        scatter_dimension=0,
        tiled=True,
    )
    picked = grad_bus[:, clipped] * weighted[None, :]
    grad_release = lax.psum(picked, "bus")
    return (grad_bus, grad_release)


def solution(mesh):
    placed = (P("br", "bus"), P("br", None), P(), P(), P("br", "bus"), P("br"), P(), P())
    return jax.shard_map(
        shards,
        mesh=mesh,
        in_specs=placed,
        out_specs=(P("br", "bus"), P("br", None)),
        check_vma=False,
    )
```

profile of v0, /device:TPU:1, one launch (start us, length us, event | category | flops | bytes accessed | tf_op | source)
XLA Modules:
  0.0 980.7 jit_solution(10808538749008123875)
XLA Ops:
  7.2 0.7 broadcast_clamp_fusion
  7.9 0.7 and_select_fusion
  8.6 0.7 multiply_bitcast_fusion.1
  9.3 0.2 copy.25
  9.6 4.7 copy.24
  14.3 11.7 %scatter_fusion = f32[2,15104]{0,1:T(8,128)} fusion(f32[2,15104]{0,1:T(8,128)} %copy.24, s32[1024]{0:T(1024)S(1)} %get-tuple-element.13, f32[1024,2]{1,0:T(8,128)S(1)} %copy.25), kind=kCustom, calls=%fused_computation.1 | custom fusion | flops 2048 | bytes 28672 | tf_op jit(solution)/shard_map/scatter-add | solution.py:19
  26.0 4.7 convert_bitcast_fusion
  30.7 4.1 copy.26
  34.8 0.0 all-reduce.4.cloned.1.call-start
  34.9 126.9 %all-gather.3.cloned.1.call-done = bf16[64,2,15104]{2,1,0:T(2,128)(2,1)} async-done(((bf16[1,2,15104]{2,1,0:T(2,128)(2,1)}), bf16[64,2,15104]{2,1,0:T(2,128)(2,1)}) %all-gather.3.cloned.1.call-update) | async-done | bytes 3866640 | tf_op jit(solution)/shard_map/all_gather | solution.py:23
  161.8 8.2 reshape.29
  170.0 5.1 fusion.7
  175.2 0.1 select_reduce_fusion.1
  175.3 40.9 %all-reduce.4.cloned.1.call-done = f32[128,128]{1,0:T(8,128)} async-done(((f32[128,128]{1,0:T(8,128)}), f32[128,128]{1,0:T(8,128)}) %all-reduce.4.cloned.1.call-update) | async-done | bytes 65552 | tf_op jit(solution)/shard_map/psum | solution.py:33
  216.1 6.4 fusion
  222.5 0.6 copy-done.4
  223.2 0.6 dynamic-slice
  224.4 681.7 %all-reduce.6.cloned.1.call-done = f32[128,15104]{1,0:T(8,128)} async-done(((f32[128,15104]{1,0:T(8,128)}), f32[128,15104]{1,0:T(8,128)}) %all-reduce.6.cloned.1.call-update) | async-done | bytes 7733264
  906.1 1.1 constant_dynamic-slice_fusion
  907.2 4.7 copy.27
  911.9 6.0 gather_fusion
  918.0 0.2 multiply_bitcast_fusion
  918.2 55.2 %psum.15 = f32[2,1024]{0,1:T(8,128)S(1)} all-reduce(f32[2,1024]{0,1:T(8,128)S(1)} %multiply_bitcast_fusion), channel_id=1, replica_groups=mesh['br'=64,'bus'=4] {'bus'}, use_global_device_ids=true, to_apply=%region_5.6 | all-reduce | flops 2048 | bytes 16384 | tf_op jit(solution)/shard_map/psum | solution.py:44
  973.4 0.8 copy.28
  (14 shorter events, 0.1 us)
Async XLA Ops:
  7.2 154.6 %all-gather.3.cloned.1.call-start = ((), (), s32[]{:S(2)}) async-start(), calls=%async_computation.1 | async-start | bytes 3927040 | tf_op jit(solution)/shard_map/all_gather | solution.py:23
  34.8 181.3 %all-reduce.4.cloned.1.call-start = ((), (), s32[]{:S(2)}) async-start(), calls=%async_computation | async-start | bytes 131072 | tf_op jit(solution)/shard_map/psum | solution.py:33
  170.0 5.2 copy-start.1
  170.0 5.2 copy-start.2
  170.0 5.2 copy-start.3
  175.1 731.0 %all-reduce.6.cloned.1.call-start = ((), (), s32[]{:S(2)}) async-start(), calls=%async_computation.2 | async-start | bytes 15466496
  222.5 0.7 copy-start.4
  907.2 4.7 copy-start
Sparse Core Ops, SparseCore 0:
  35.0 126.7 all-gather.2
  175.2 40.8 all-reduce.3
  222.7 683.4 all-reduce.5
where the time goes:
time: 981 us
  waiting for transfers between devices  849 us (87%)
  blocking collectives  55.2 us (6%)
  local copies, waits for them, and re-layouts  31.2 us (3%)
  other arithmetic  18.8 us (2%)
  between operations  14.5 us (1%)
  matrix products  11.5 us (1%)
    unnamed x4, waiting for transfers between devices  682 us
    all_gather x1, waiting for transfers between devices, shards(): lax.all_gather(inject, 'br', axis=0, tiled=True)  127 us
    psum x1, blocking collectives, shards(): grad_release = lax.psum(picked, 'bus')  55.2 us
    psum x1, waiting for transfers between devices, shards(): flows = lax.psum(partial_flows, 'bus')  40.9 us
  transfers between devices with their start and end apart: 3, of which 3 were waited for; matrix products, arithmetic and copies ran while one was open for 0% of the time, Pallas kernels for 0%

commit v1 on v0

--- a/solution.py
+++ b/solution.py
@@ -41,7 +41,7 @@
         tiled=True,
     )
     picked = grad_bus[:, clipped] * weighted[None, :]
-    grad_release = lax.psum(picked, "bus")
+    grad_release = jnp.sum(lax.all_gather(picked, "bus"), axis=0)
     return (grad_bus, grad_release)
 
 

time: 981 us -> 972 us (level)
    psum x1 -> x0, blocking collectives: 55.2 us -> none  [shards(): grad_release = lax.psum(picked, 'bus')]
    all_gather x0 -> x1, blocking collectives: none -> 46 us  [shards(): grad_release = jnp.sum(lax.all_gather(picked, 'bus'), axis=0)]
where the time goes in v1:
time: 972 us
  waiting for transfers between devices  849 us (87%)
  blocking collectives  46 us (5%)
  local copies, waits for them, and re-layouts  30.6 us (3%)
  other arithmetic  19.4 us (2%)
  between operations  14.5 us (1%)
  matrix products  11.5 us (1%)
    unnamed x4, waiting for transfers between devices  682 us
    all_gather x1, waiting for transfers between devices, shards(): lax.all_gather(inject, 'br', axis=0, tiled=True)  127 us
    all_gather x1, blocking collectives, shards(): grad_release = jnp.sum(lax.all_gather(picked, 'bus'), axis=0)  46 us
    psum x1, waiting for transfers between devices, shards(): flows = lax.psum(partial_flows, 'bus')  40.9 us
  transfers between devices with their start and end apart: 3, of which 3 were waited for; matrix products, arithmetic and copies ran while one was open for 0% of the time, Pallas kernels for 0%

profile of v1, /device:TPU:1, one launch (start us, length us, event | category | flops | bytes accessed | tf_op | source)
XLA Modules:
  0.0 971.5 jit_solution(7856487809785804437)
XLA Ops:
  7.2 0.7 broadcast_clamp_fusion
  7.9 0.7 and_select_fusion
  8.6 0.7 multiply_bitcast_fusion
  9.3 0.2 copy.25
  9.6 4.7 copy.24
  14.3 11.7 %scatter_fusion = f32[2,15104]{0,1:T(8,128)} fusion(f32[2,15104]{0,1:T(8,128)} %copy.24, s32[1024]{0:T(1024)S(1)} %get-tuple-element.9, f32[1024,2]{1,0:T(8,128)S(1)} %copy.25), kind=kCustom, calls=%fused_computation.1 | custom fusion | flops 2048 | bytes 28672 | tf_op jit(solution)/shard_map/scatter-add | solution.py:19
  26.0 4.7 convert_bitcast_fusion
  30.7 4.1 copy.26
  34.9 126.9 %all-gather.3.cloned.1.call-done = bf16[64,2,15104]{2,1,0:T(2,128)(2,1)} async-done(((bf16[1,2,15104]{2,1,0:T(2,128)(2,1)}), bf16[64,2,15104]{2,1,0:T(2,128)(2,1)}) %all-gather.3.cloned.1.call-update) | async-done | bytes 3866640 | tf_op jit(solution)/shard_map/all_gather | solution.py:23
  161.8 8.2 reshape.56
  170.0 5.1 fusion.7
  175.2 0.1 select_reduce_fusion.1
  175.3 40.9 %all-reduce.4.cloned.1.call-done = f32[128,128]{1,0:T(8,128)} async-done(((f32[128,128]{1,0:T(8,128)}), f32[128,128]{1,0:T(8,128)}) %all-reduce.4.cloned.1.call-update) | async-done | bytes 65552 | tf_op jit(solution)/shard_map/psum | solution.py:33
  216.1 6.4 fusion
  222.5 0.6 copy-done.4
  223.2 0.6 dynamic-slice
  224.4 681.7 %all-reduce.6.cloned.1.call-done = f32[128,15104]{1,0:T(8,128)} async-done(((f32[128,15104]{1,0:T(8,128)}), f32[128,15104]{1,0:T(8,128)}) %all-reduce.6.cloned.1.call-update) | async-done | bytes 7733264
  906.1 1.1 constant_dynamic-slice_fusion
  907.2 4.7 copy.27
  911.9 6.0 gather_fusion
  918.0 0.2 bitcast_multiply_fusion
  918.2 0.2 copy.28
  918.3 46.0 %all_gather.8 = f32[4,2,1024]{2,1,0:T(2,128)S(1)} all-gather(f32[1,2,1024]{2,1,0:T(2,128)S(1)} %copy.28), channel_id=1, replica_groups=mesh['br'=64,'bus'=4] {'bus'}, dimensions={0}, use_global_device_ids=true | all-gather | bytes 40960 | tf_op jit(solution)/shard_map/all_gather | solution.py:44
  964.4 0.6 reduce_sum.29
  (15 shorter events, 0.2 us)
Async XLA Ops:
  7.2 154.6 %all-gather.3.cloned.1.call-start = ((), (), s32[]{:S(2)}) async-start(), calls=%async_computation.1 | async-start | bytes 3927040 | tf_op jit(solution)/shard_map/all_gather | solution.py:23
  34.8 181.3 %all-reduce.4.cloned.1.call-start = ((), (), s32[]{:S(2)}) async-start(), calls=%async_computation | async-start | bytes 131072 | tf_op jit(solution)/shard_map/psum | solution.py:33
  170.0 5.2 copy-start.1
  170.0 5.2 copy-start.2
  170.0 5.2 copy-start.3
  175.1 731.0 %all-reduce.6.cloned.1.call-start = ((), (), s32[]{:S(2)}) async-start(), calls=%async_computation.2 | async-start | bytes 15466496
  222.5 0.7 copy-start.4
  907.2 4.7 copy-start
Sparse Core Ops, SparseCore 0:
  35.0 126.7 all-gather.2
  175.2 40.8 all-reduce.3
  222.7 683.4 all-reduce.5
